TPU v7x, 32 devices: a whole 2x2x4 slice. The times are simulated.
32 devices in a mesh: groups: 2 (over y), feat: 4 (over z), layer: 2 (over x), tok: 2 (over core).
Axes of the slice: x: 2, y: 2, z: 4, core: 2. Of those that a mesh axis runs over, the one named last changes fastest.
Arguments:
- residual_in: float32 [256, 2, 1792], P('groups', 'tok', 'feat'), parts along dimension 0, may hold values from -6 to 6
- attn_scale: float32 [2, 256], P('layer', 'groups'), parts along dimension 1, may hold values from 0.4 to 2.5
- mlp_scale: float32 [2, 256], P('layer', 'groups'), parts along dimension 1, may hold values from 0.4 to 2.5
- patterns: bfloat16 [2, 8, 4, 64, 64], P('layer', None, 'groups'), parts along dimension 2, may hold values from 0.0029907227 to 0.059814453
- lengths: int32 [4], P('groups'), parts along dimension 0, may hold values from 16 to 64
- value_proj: bfloat16 [2, 2, 1792, 1024], P('layer', 'tok', None, 'feat'), may hold values from -0.09375 to 0.09375
- out_proj: bfloat16 [2, 4, 256, 2, 2, 1792], P('layer', None, None, None, 'tok', 'feat'), may hold values from -0.125 to 0.125
- enc_weight: bfloat16 [2, 2, 1792, 512], P('layer', 'tok', None, 'feat'), may hold values from -0.09375 to 0.09375
- enc_bias: float32 [2, 512], P('layer', 'feat'), may hold values from -3 to 3
- dec_weight: bfloat16 [2, 2, 512, 2, 1792], P('layer', None, None, 'tok', 'feat'), may hold values from -0.25 to 0.25
- errors: float32 [2, 256, 2, 1792], P('layer', 'groups', 'tok', 'feat'), parts along dimension 1, may hold values from -4 to 4
- clamp_mode: int32 [2, 16384], P('layer', 'feat'), may hold values from 0 to 2
- clamp_index: int32 [2, 16384], P('layer', 'feat'), may hold values from 0 to 63
- clamp_values: float32 [64], replicated, may hold values from 0.25 to 3
- active_blocks: int32 [2, 4], P('layer', 'feat'), may hold values from 0 to 31
Outputs:
- residual_out: float32 [2, 256, 2, 1792], P('layer', 'groups', 'tok', 'feat'), parts along dimension 1
- features: bfloat16 [2, 256, 512], P('layer', 'groups', 'feat'), parts along dimension 1
There are 2 independent parts, one for each index of `groups`. A program takes and returns all parts, laid end to end along the dimension named above; an argument that names none is the same for every part. Nothing has to cross between parts.
Inputs may be any that keep to these rules, and one draw needn't show every extreme that they name: `clamp_mode`: 0 leaves a feature free, 1 sets it to its table value, 2 multiplies it by its table value. `lengths`: positions at or past a prompt's length are padding.
All inputs are finite; a program needn't handle non-finite values.
Results may differ from a plain program's by a relative error of at most 0.018.
Values may be sent and summed in bfloat16 or wider, within the bound.
A program may use at most 64 MiB of HBM per device.

v0:
```python
import jax
import jax.numpy as jnp
from jax import lax
from jax.sharding import PartitionSpec as P


def passed_along(value, axis, steps):
    count = lax.axis_size(axis)
    initial, last = (max(0, -steps), min(count, count - steps))
    return lax.ppermute(value, axis, [(source, source + steps) for source in range(initial, last)])


def columns(normed_rows):
    return lax.all_gather(normed_rows, "feat", axis=1, tiled=True)


def halves(partial_sum):
    return lax.psum(partial_sum, "tok")


def pick_block(lookup_table, chosen, block_len):
    shaped = lookup_table.reshape(-1, block_len)
    return lax.dynamic_slice_in_dim(shaped, chosen, 1, 0)[0]


def local(
    residual_in,
    attn_scale,
    mlp_scale,
    patterns,
    lengths,
    value_proj,
    out_proj,
    enc_weight,
    enc_bias,
    dec_weight,
    errors,
    clamp_mode,
    clamp_index,
    clamp_values,
    active_blocks,
):
    layer_count = lax.axis_size("layer")
    my_layer = lax.axis_index("layer")
    my_range = lax.axis_index("feat")
    seq_len = patterns.shape[3]
    prompt_count = patterns.shape[2]
    head_dim = out_proj.shape[2]
    per_group = out_proj.shape[3]
    kv_cols = value_proj.shape[3]
    width_cols = residual_in.shape[2]
    block_len = enc_bias.shape[1]
    total_rows = residual_in.shape[0]
    split_count = 1
    block_rows = seq_len // split_count
    micro_count = prompt_count * split_count
    section_count = layer_count + micro_count - 1
    source_rows = residual_in[:, 0, :]
    error_rows = errors[0, :, 0, :]
    value_weight = value_proj[0, 0]
    out_weight = out_proj[0].reshape(-1, width_cols)
    enc_rows = enc_weight[0, 0]
    enc_shift = enc_bias[0]
    dec_rows = dec_weight[0, :, :, 0, :]
    chosen = active_blocks[0, 0]
    modes = pick_block(clamp_mode[0], chosen, block_len)
    table_pick = pick_block(clamp_index[0], chosen, block_len)
    table_ids = jnp.arange(clamp_values.shape[0], dtype=jnp.int32)
    levels = jnp.sum(
        jnp.where(table_pick[:, None] == table_ids[None, :], clamp_values[None, :], 0.0), axis=1
    )
    group_id = my_range * kv_cols // head_dim
    group_pat = lax.dynamic_slice_in_dim(patterns[0], group_id * per_group, per_group, 0)
    positions = jnp.arange(seq_len, dtype=jnp.int32)
    scale_attn = attn_scale[0]
    scale_mlp = mlp_scale[0]

    def add_heads(piece):
        return jnp.dot(piece, out_weight, preferred_element_type=jnp.float32)

    def add_writes(piece):
        return jnp.einsum("rf,tfc->trc", piece, dec_rows, preferred_element_type=jnp.float32)

    def section(step_num, carry):
        recv_rows, links, value_cache, kept_rows, kept_feats = carry
        micro_raw = step_num - my_layer
        is_live = (micro_raw >= 0) & (micro_raw < micro_count)
        micro_num = jnp.clip(micro_raw, 0, micro_count - 1)
        prompt_num = micro_num // split_count
        block_num = micro_num % split_count
        first_row = micro_num * block_rows
        first_pos = block_num * block_rows
        start_rows = lax.dynamic_slice_in_dim(source_rows, first_row, block_rows, 0)
        rows_in = jnp.where(my_layer == 0, start_rows, recv_rows)
        row_attn = lax.dynamic_slice_in_dim(scale_attn, first_row, block_rows, 0)
        normed = (rows_in * row_attn[:, None]).astype(jnp.bfloat16)
        values = halves(
            jnp.dot(columns(normed), value_weight, preferred_element_type=jnp.float32)
        ).astype(jnp.bfloat16)
        value_cache = values
        query_pos = first_pos + jnp.arange(block_rows, dtype=jnp.int32)
        prompt_len = lax.dynamic_index_in_dim(lengths, prompt_num, 0, keepdims=False)
        keep_keys = (positions[None, :] <= query_pos[:, None]) & (positions[None, :] < prompt_len)
        block_pat = lax.dynamic_slice(
            group_pat, (0, prompt_num, first_pos, 0), (per_group, 1, block_rows, seq_len)
        )[:, 0]
        block_pat = jnp.where(keep_keys[None], block_pat, jnp.zeros_like(block_pat))
        head_out = (
            jnp.einsum("uqk,kc->qcu", block_pat, value_cache, preferred_element_type=jnp.float32)
            .astype(jnp.bfloat16)
            .reshape(block_rows, -1)
        )
        attention = add_heads(lax.all_gather(head_out, "feat", axis=1, tiled=True))
        middle = rows_in + attention
        row_mlp = lax.dynamic_slice_in_dim(scale_mlp, first_row, block_rows, 0)
        normed_mlp = (middle * row_mlp[:, None]).astype(jnp.bfloat16)
        preact = (
            halves(jnp.dot(columns(normed_mlp), enc_rows, preferred_element_type=jnp.float32))
            + enc_shift
        )
        active = jnp.maximum(preact, 0.0)
        clamped = jnp.where(modes == 1, levels, jnp.where(modes == 2, active * levels, active))
        live_rows = query_pos < prompt_len
        block_feats = jnp.where(live_rows[:, None], clamped, 0.0).astype(jnp.bfloat16)
        writes = add_writes(lax.all_gather(block_feats, "feat", axis=1, tiled=True))
        error_block = lax.dynamic_slice_in_dim(error_rows, first_row, block_rows, 0)
        acc_in = jnp.where(my_layer == 0, jnp.zeros_like(links), links)
        running = acc_in + writes
        recon = lax.dynamic_index_in_dim(running, my_layer, 0, keepdims=False)
        rows_next = middle + recon + error_block
        recv_rows, links = passed_along((rows_next, running), "layer", 1)
        old_rows = lax.dynamic_slice_in_dim(kept_rows, first_row, block_rows, 0)
        kept_rows = lax.dynamic_update_slice_in_dim(
            kept_rows, jnp.where(is_live, rows_next, old_rows), first_row, 0
        )
        old_feats = lax.dynamic_slice_in_dim(kept_feats, first_row, block_rows, 0)
        kept_feats = lax.dynamic_update_slice_in_dim(
            kept_feats, jnp.where(is_live, block_feats, old_feats), first_row, 0
        )
        return (recv_rows, links, value_cache, kept_rows, kept_feats)

    link_start = jnp.zeros((layer_count, block_rows, width_cols), jnp.float32)
    initial = (
        jnp.zeros((block_rows, width_cols), jnp.float32),
        link_start,
        jnp.zeros((seq_len, kv_cols), jnp.bfloat16),
        jnp.zeros((total_rows, width_cols), jnp.float32),
        jnp.zeros((total_rows, block_len), jnp.bfloat16),
    )
    final = lax.fori_loop(0, section_count, section, initial)
    return (final[3][None, :, None, :], final[4][None])


def solution(mesh):
    return jax.shard_map(
        local,
        mesh=mesh,
        in_specs=(
            P("groups", "tok", "feat"),
            P("layer", "groups"),
            P("layer", "groups"),
            P("layer", None, "groups", None, None),
            P("groups"),
            P("layer", "tok", None, "feat"),
            P("layer", None, None, None, "tok", "feat"),
            P("layer", "tok", None, "feat"),
            P("layer", "feat"),
            P("layer", None, None, "tok", "feat"),
            P("layer", "groups", "tok", "feat"),
            P("layer", "feat"),
            P("layer", "feat"),
            P(),
            P("layer", "feat"),
        ),
        out_specs=(P("layer", "groups", "tok", "feat"), P("layer", "groups", "feat")),
        check_vma=False,
    )
```

profile of v0, /device:TPU:0, one launch (start us, length us, event | category | flops | bytes accessed | tf_op | source)
XLA Modules:
  0.0 265.3 jit_solution(8046609144955655287)
XLA Ops:
  0.7 0.9 copy-done
  2.2 0.7 fusion.19
  3.0 0.7 select_reduce_fusion
  3.7 6.1 %copy.43 = bf16[1,4,256,2,1,448]{5,3,2,1,4,0:T(2,128)(2,1)} copy(bf16[1,4,256,2,1,448]{2,5,4,3,1,0:T(8,128)(2,1)} %param.23) | data formatting | bytes 3670016 | tf_op args[6]
  9.9 3.5 %reshape_squeeze.9 = bf16[2048,448]{1,0:T(8,128)(2,1)S(1)} reshape(bf16[1,4,256,2,1,448]{5,3,2,1,4,0:T(2,128)(2,1)} %copy.43) | data formatting | bytes 3670016 | tf_op jit(solution)/shard_map/reshape;squeeze | solution.py:61
  13.5 0.8 copy.44
  14.4 0.7 broadcast.116
  15.1 0.7 broadcast_in_dim.131
  15.9 247.6 %while.23 = (s32[]{:T(128)}, f32[64,448]{1,0:T(8,128)S(1)}, f32[2,64,448]{2,1,0:T(8,128)}, f32[128,448]{1,0:T(8,128)}, bf16[128,128]{1,0:T(8,128)(2,1)S(1)}, /*i...) while((s32[]{:T(128)}, f32[64,448]{1,0:T(8,128)S(1)}, ...), condition=%wide.region_4.5_spmd.clone.clone, body=%wide.region_1.4_spmd.clone.clone.sunk | while | flops 268976448 | bytes 11732813 | solution.py:150
  16.1 15.7 %all-gather.6 = bf16[4,448,64]{1,2,0:T(8,128)(2,1)S(1)} all-gather(bf16[1,448,64]{1,2,0:T(8,128)(2,1)S(1)} %fusion.57), channel_id=1, replica_groups=mesh['groups'=2,'feat'=4,'layer'=2,'tok'=2] {'feat'}, dimensions={0}, use_global_device_ids=true | all-gather | bytes 286720 | tf_op jit(solution)/shard_map/while/body/eval_jaxpr/all_gather | solution.py:14
  31.9 0.3 reshape.85
  32.2 1.5 fusion.58
  33.7 3.6 %psum.34 = bf16[64,256]{1,0:T(8,128)(2,1)S(1)} all-reduce(f32[64,256]{1,0:T(8,128)S(1)} %fusion.58), channel_id=1, replica_groups=mesh['groups'=2,'feat'=4,'layer'=2,'tok'=2] {'tok'}, use_global_device_ids=true, to_apply=%region_2.2 | all-reduce | flops 16384 | bytes 98304 | tf_op jit(solution)/shard_map/while/body/eval_jaxpr/psum | solution.py:18
  37.3 0.7 dynamic_slice.163
  37.9 0.7 iota_compare_fusion.4
  38.9 16.6 %all_gather.48 = bf16[64,2048]{0,1:T(8,128)(2,1)S(1)} all-gather(bf16[64,512]{0,1:T(8,128)(2,1)S(1)} %bitcast.101), channel_id=1, replica_groups=mesh['groups'=2,'feat'=4,'layer'=2,'tok'=2] {'feat'}, dimensions={1}, use_global_device_ids=true | all-gather | bytes 327680 | tf_op jit(solution)/shard_map/while/body/eval_jaxpr/all_gather | solution.py:113
  55.6 0.5 convolution_add_fusion.2
  56.2 14.5 %all-gather.7 = bf16[4,448,64]{1,2,0:T(8,128)(2,1)S(1)} all-gather(bf16[1,448,64]{1,2,0:T(8,128)(2,1)S(1)} %fusion.61), channel_id=1, replica_groups=mesh['groups'=2,'feat'=4,'layer'=2,'tok'=2] {'feat'}, dimensions={0}, use_global_device_ids=true | all-gather | bytes 286720 | tf_op jit(solution)/shard_map/while/body/eval_jaxpr/all_gather | solution.py:14
  70.9 0.3 reshape.86
  71.2 1.2 fusion.62
  72.4 3.4 %psum.35 = f32[64,128]{1,0:T(8,128)S(1)} all-reduce(f32[64,128]{1,0:T(8,128)S(1)} %fusion.62), channel_id=1, replica_groups=mesh['groups'=2,'feat'=4,'layer'=2,'tok'=2] {'tok'}, use_global_device_ids=true, to_apply=%region_3.3 | all-reduce | flops 8192 | bytes 65536 | tf_op jit(solution)/shard_map/while/body/eval_jaxpr/psum | solution.py:18
  76.0 12.0 %all_gather.49 = bf16[64,512]{1,0:T(8,128)(2,1)S(1)} all-gather(bf16[64,128]{1,0:T(8,128)(2,1)S(1)} %get-tuple-element.762), channel_id=1, replica_groups=mesh['groups'=2,'feat'=4,'layer'=2,'tok'=2] {'feat'}, dimensions={1}, use_global_device_ids=true | all-gather | bytes 81920 | tf_op jit(solution)/shard_map/while/body/eval_jaxpr/all_gather | solution.py:125
  88.0 1.6 fusion.63
  89.5 4.1 %collective-permute-start.1 = (f32[2,64,448]{2,1,0:T(8,128)S(1)}, f32[2,64,448]{2,1,0:T(8,128)}, u32[]{:S(2)}, u32[]{:S(2)}) collective-permute-start(f32[2,64,448]{2,1,0:T(8,128)S(1)} %fusion.63), channel_id=1, source_target_pairs={{0,2},{1,3},{4,6},{5,7},{8,10},{9,11},{12,14},{13,15},{16,18},{17,... | collective-permute-start | bytes 688136 | tf_op jit(solution)/shard_map/while/body/eval_jaxpr/ppermute | solution.py:10
  93.7 1.6 select_dynamic-update-slice_fusion.5
  95.3 1.3 collective-permute-start
  96.6 3.0 %collective-permute-done = f32[64,448]{1,0:T(8,128)S(1)} collective-permute-done((f32[64,448]{1,0:T(8,128)S(1)}, f32[64,448]{1,0:T(8,128)S(1)}, u32[]{:S(2)}, u32[]{:S(2)}) %collective-permute-start) | collective-permute-done | bytes 114720 | tf_op jit(solution)/shard_map/while/body/eval_jaxpr/ppermute | solution.py:10
  99.8 14.3 %all-gather.6 = bf16[4,448,64]{1,2,0:T(8,128)(2,1)S(1)} all-gather(bf16[1,448,64]{1,2,0:T(8,128)(2,1)S(1)} %fusion.57), channel_id=1, replica_groups=mesh['groups'=2,'feat'=4,'layer'=2,'tok'=2] {'feat'}, dimensions={0}, use_global_device_ids=true | all-gather | bytes 286720 | tf_op jit(solution)/shard_map/while/body/eval_jaxpr/all_gather | solution.py:14
  114.3 0.3 reshape.85
  114.6 1.5 fusion.58
  116.1 3.6 %psum.34 = bf16[64,256]{1,0:T(8,128)(2,1)S(1)} all-reduce(f32[64,256]{1,0:T(8,128)S(1)} %fusion.58), channel_id=1, replica_groups=mesh['groups'=2,'feat'=4,'layer'=2,'tok'=2] {'tok'}, use_global_device_ids=true, to_apply=%region_2.2 | all-reduce | flops 16384 | bytes 98304 | tf_op jit(solution)/shard_map/while/body/eval_jaxpr/psum | solution.py:18
  119.7 0.7 dynamic_slice.163
  120.3 0.7 iota_compare_fusion.4
  121.3 16.2 %all_gather.48 = bf16[64,2048]{0,1:T(8,128)(2,1)S(1)} all-gather(bf16[64,512]{0,1:T(8,128)(2,1)S(1)} %bitcast.101), channel_id=1, replica_groups=mesh['groups'=2,'feat'=4,'layer'=2,'tok'=2] {'feat'}, dimensions={1}, use_global_device_ids=true | all-gather | bytes 327680 | tf_op jit(solution)/shard_map/while/body/eval_jaxpr/all_gather | solution.py:113
  137.6 0.5 convolution_add_fusion.2
  138.2 13.8 %all-gather.7 = bf16[4,448,64]{1,2,0:T(8,128)(2,1)S(1)} all-gather(bf16[1,448,64]{1,2,0:T(8,128)(2,1)S(1)} %fusion.61), channel_id=1, replica_groups=mesh['groups'=2,'feat'=4,'layer'=2,'tok'=2] {'feat'}, dimensions={0}, use_global_device_ids=true | all-gather | bytes 286720 | tf_op jit(solution)/shard_map/while/body/eval_jaxpr/all_gather | solution.py:14
  152.2 0.3 reshape.86
  152.5 1.2 fusion.62
  153.7 3.4 %psum.35 = f32[64,128]{1,0:T(8,128)S(1)} all-reduce(f32[64,128]{1,0:T(8,128)S(1)} %fusion.62), channel_id=1, replica_groups=mesh['groups'=2,'feat'=4,'layer'=2,'tok'=2] {'tok'}, use_global_device_ids=true, to_apply=%region_3.3 | all-reduce | flops 8192 | bytes 65536 | tf_op jit(solution)/shard_map/while/body/eval_jaxpr/psum | solution.py:18
  157.3 12.0 %all_gather.49 = bf16[64,512]{1,0:T(8,128)(2,1)S(1)} all-gather(bf16[64,128]{1,0:T(8,128)(2,1)S(1)} %get-tuple-element.762), channel_id=1, replica_groups=mesh['groups'=2,'feat'=4,'layer'=2,'tok'=2] {'feat'}, dimensions={1}, use_global_device_ids=true | all-gather | bytes 81920 | tf_op jit(solution)/shard_map/while/body/eval_jaxpr/all_gather | solution.py:125
  169.3 1.6 fusion.63
  170.8 5.0 %collective-permute-start.1 = (f32[2,64,448]{2,1,0:T(8,128)S(1)}, f32[2,64,448]{2,1,0:T(8,128)}, u32[]{:S(2)}, u32[]{:S(2)}) collective-permute-start(f32[2,64,448]{2,1,0:T(8,128)S(1)} %fusion.63), channel_id=1, source_target_pairs={{0,2},{1,3},{4,6},{5,7},{8,10},{9,11},{12,14},{13,15},{16,18},{17,... | collective-permute-start | bytes 688136 | tf_op jit(solution)/shard_map/while/body/eval_jaxpr/ppermute | solution.py:10
  175.9 1.7 select_dynamic-update-slice_fusion.5
  177.5 1.3 collective-permute-start
  178.8 3.0 %collective-permute-done = f32[64,448]{1,0:T(8,128)S(1)} collective-permute-done((f32[64,448]{1,0:T(8,128)S(1)}, f32[64,448]{1,0:T(8,128)S(1)}, u32[]{:S(2)}, u32[]{:S(2)}) %collective-permute-start) | collective-permute-done | bytes 114720 | tf_op jit(solution)/shard_map/while/body/eval_jaxpr/ppermute | solution.py:10
  182.0 13.8 %all-gather.6 = bf16[4,448,64]{1,2,0:T(8,128)(2,1)S(1)} all-gather(bf16[1,448,64]{1,2,0:T(8,128)(2,1)S(1)} %fusion.57), channel_id=1, replica_groups=mesh['groups'=2,'feat'=4,'layer'=2,'tok'=2] {'feat'}, dimensions={0}, use_global_device_ids=true | all-gather | bytes 286720 | tf_op jit(solution)/shard_map/while/body/eval_jaxpr/all_gather | solution.py:14
  196.0 0.3 reshape.85
  196.3 1.5 fusion.58
  197.7 3.6 %psum.34 = bf16[64,256]{1,0:T(8,128)(2,1)S(1)} all-reduce(f32[64,256]{1,0:T(8,128)S(1)} %fusion.58), channel_id=1, replica_groups=mesh['groups'=2,'feat'=4,'layer'=2,'tok'=2] {'tok'}, use_global_device_ids=true, to_apply=%region_2.2 | all-reduce | flops 16384 | bytes 98304 | tf_op jit(solution)/shard_map/while/body/eval_jaxpr/psum | solution.py:18
  201.4 0.7 dynamic_slice.163
  202.0 0.7 iota_compare_fusion.4
  203.0 16.1 %all_gather.48 = bf16[64,2048]{0,1:T(8,128)(2,1)S(1)} all-gather(bf16[64,512]{0,1:T(8,128)(2,1)S(1)} %bitcast.101), channel_id=1, replica_groups=mesh['groups'=2,'feat'=4,'layer'=2,'tok'=2] {'feat'}, dimensions={1}, use_global_device_ids=true | all-gather | bytes 327680 | tf_op jit(solution)/shard_map/while/body/eval_jaxpr/all_gather | solution.py:113
  219.1 0.5 convolution_add_fusion.2
  219.7 13.8 %all-gather.7 = bf16[4,448,64]{1,2,0:T(8,128)(2,1)S(1)} all-gather(bf16[1,448,64]{1,2,0:T(8,128)(2,1)S(1)} %fusion.61), channel_id=1, replica_groups=mesh['groups'=2,'feat'=4,'layer'=2,'tok'=2] {'feat'}, dimensions={0}, use_global_device_ids=true | all-gather | bytes 286720 | tf_op jit(solution)/shard_map/while/body/eval_jaxpr/all_gather | solution.py:14
  233.8 0.3 reshape.86
  234.0 1.2 fusion.62
  235.3 3.4 %psum.35 = f32[64,128]{1,0:T(8,128)S(1)} all-reduce(f32[64,128]{1,0:T(8,128)S(1)} %fusion.62), channel_id=1, replica_groups=mesh['groups'=2,'feat'=4,'layer'=2,'tok'=2] {'tok'}, use_global_device_ids=true, to_apply=%region_3.3 | all-reduce | flops 8192 | bytes 65536 | tf_op jit(solution)/shard_map/while/body/eval_jaxpr/psum | solution.py:18
  238.8 12.0 %all_gather.49 = bf16[64,512]{1,0:T(8,128)(2,1)S(1)} all-gather(bf16[64,128]{1,0:T(8,128)(2,1)S(1)} %get-tuple-element.762), channel_id=1, replica_groups=mesh['groups'=2,'feat'=4,'layer'=2,'tok'=2] {'feat'}, dimensions={1}, use_global_device_ids=true | all-gather | bytes 81920 | tf_op jit(solution)/shard_map/while/body/eval_jaxpr/all_gather | solution.py:125
  250.8 1.6 fusion.63
  252.4 5.1 %collective-permute-start.1 = (f32[2,64,448]{2,1,0:T(8,128)S(1)}, f32[2,64,448]{2,1,0:T(8,128)}, u32[]{:S(2)}, u32[]{:S(2)}) collective-permute-start(f32[2,64,448]{2,1,0:T(8,128)S(1)} %fusion.63), channel_id=1, source_target_pairs={{0,2},{1,3},{4,6},{5,7},{8,10},{9,11},{12,14},{13,15},{16,18},{17,... | collective-permute-start | bytes 688136 | tf_op jit(solution)/shard_map/while/body/eval_jaxpr/ppermute | solution.py:10
  257.5 1.7 select_dynamic-update-slice_fusion.5
  259.1 1.3 collective-permute-start
  260.4 3.0 %collective-permute-done = f32[64,448]{1,0:T(8,128)S(1)} collective-permute-done((f32[64,448]{1,0:T(8,128)S(1)}, f32[64,448]{1,0:T(8,128)S(1)}, u32[]{:S(2)}, u32[]{:S(2)}) %collective-permute-start) | collective-permute-done | bytes 114720 | tf_op jit(solution)/shard_map/while/body/eval_jaxpr/ppermute | solution.py:10
  263.5 1.8 copy.45
  (55 shorter events, 3.5 us)
Async XLA Ops:
  0.6 1.0 copy-start
  9.8 3.5 %copy-start.2 = (f32[128,1,448]{0,2,1:T(8,128)S(1)}, f32[128,1,448]{0,2,1:T(8,128)}, u32[]{:S(2)}) copy-start(f32[128,1,448]{0,2,1:T(8,128)} %param.17) | copy-start | bytes 688132
  9.8 3.7 %copy-start.3 = (f32[1,128,1,448]{1,3,2,0:T(8,128)S(1)}, f32[1,128,1,448]{1,3,2,0:T(8,128)}, u32[]{:S(2)}) copy-start(f32[1,128,1,448]{1,3,2,0:T(8,128)} %param.27) | copy-start | bytes 688132
  9.8 6.0 %copy-start.4 = (f32[1,128]{1,0:T(1,128)S(1)}, f32[1,128]{1,0:T(1,128)}, u32[]{:S(2)}) copy-start(f32[1,128]{1,0:T(1,128)} %param.25) | copy-start | bytes 1540
  9.8 6.0 %copy-start.5 = (f32[1,128]{1,0:T(1,128)S(1)}, f32[1,128]{1,0:T(1,128)}, u32[]{:S(2)}) copy-start(f32[1,128]{1,0:T(1,128)} %param.18) | copy-start | bytes 1540
  9.9 6.0 %copy-start.6 = (s32[2]{0:T(128)S(1)}, s32[2]{0:T(128)}, u32[]{:S(2)}) copy-start(s32[2]{0:T(128)} %param.21) | copy-start | bytes 28
  9.9 6.0 %copy-start.7 = (f32[1,128]{1,0:T(1,128)S(1)}, f32[1,128]{1,0:T(1,128)}, u32[]{:S(2)}) copy-start(f32[1,128]{1,0:T(1,128)} %param.19) | copy-start | bytes 1540
  89.5 10.1 %collective-permute-start.1 = (f32[2,64,448]{2,1,0:T(8,128)S(1)}, f32[2,64,448]{2,1,0:T(8,128)}, u32[]{:S(2)}, u32[]{:S(2)}) collective-permute-start(f32[2,64,448]{2,1,0:T(8,128)S(1)} %fusion.63), channel_id=1, source_target_pairs={{0,2},{1,3},{4,6},{5,7},{8,10},{9,11},{12,14},{13,15},{16,18},{17,... | collective-permute-start | bytes 688136 | tf_op jit(solution)/shard_map/while/body/eval_jaxpr/ppermute | solution.py:10
  95.3 4.3 %collective-permute-start = (f32[64,448]{1,0:T(8,128)S(1)}, f32[64,448]{1,0:T(8,128)S(1)}, u32[]{:S(2)}, u32[]{:S(2)}) collective-permute-start(f32[64,448]{1,0:T(8,128)S(1)} %get-tuple-element.763), channel_id=1, source_target_pairs={{0,2},{1,3},{4,6},{5,7},{8,10},{9,11},{12,14},{13,15},{16,18},{17,... | collective-permute-start | bytes 344072 | tf_op jit(solution)/shard_map/while/body/eval_jaxpr/ppermute | solution.py:10
  170.8 11.0 %collective-permute-start.1 = (f32[2,64,448]{2,1,0:T(8,128)S(1)}, f32[2,64,448]{2,1,0:T(8,128)}, u32[]{:S(2)}, u32[]{:S(2)}) collective-permute-start(f32[2,64,448]{2,1,0:T(8,128)S(1)} %fusion.63), channel_id=1, source_target_pairs={{0,2},{1,3},{4,6},{5,7},{8,10},{9,11},{12,14},{13,15},{16,18},{17,... | collective-permute-start | bytes 688136 | tf_op jit(solution)/shard_map/while/body/eval_jaxpr/ppermute | solution.py:10
  177.5 4.3 %collective-permute-start = (f32[64,448]{1,0:T(8,128)S(1)}, f32[64,448]{1,0:T(8,128)S(1)}, u32[]{:S(2)}, u32[]{:S(2)}) collective-permute-start(f32[64,448]{1,0:T(8,128)S(1)} %get-tuple-element.763), channel_id=1, source_target_pairs={{0,2},{1,3},{4,6},{5,7},{8,10},{9,11},{12,14},{13,15},{16,18},{17,... | collective-permute-start | bytes 344072 | tf_op jit(solution)/shard_map/while/body/eval_jaxpr/ppermute | solution.py:10
  252.4 11.1 %collective-permute-start.1 = (f32[2,64,448]{2,1,0:T(8,128)S(1)}, f32[2,64,448]{2,1,0:T(8,128)}, u32[]{:S(2)}, u32[]{:S(2)}) collective-permute-start(f32[2,64,448]{2,1,0:T(8,128)S(1)} %fusion.63), channel_id=1, source_target_pairs={{0,2},{1,3},{4,6},{5,7},{8,10},{9,11},{12,14},{13,15},{16,18},{17,... | collective-permute-start | bytes 688136 | tf_op jit(solution)/shard_map/while/body/eval_jaxpr/ppermute | solution.py:10
  259.1 4.3 %collective-permute-start = (f32[64,448]{1,0:T(8,128)S(1)}, f32[64,448]{1,0:T(8,128)S(1)}, u32[]{:S(2)}, u32[]{:S(2)}) collective-permute-start(f32[64,448]{1,0:T(8,128)S(1)} %get-tuple-element.763), channel_id=1, source_target_pairs={{0,2},{1,3},{4,6},{5,7},{8,10},{9,11},{12,14},{13,15},{16,18},{17,... | collective-permute-start | bytes 344072 | tf_op jit(solution)/shard_map/while/body/eval_jaxpr/ppermute | solution.py:10
  263.5 1.8 copy-start.1
where the time goes:
time: 266 us; the launch traced here: 265 us
  blocking collectives  192 us (72%)
  local copies, waits for them, and re-layouts  21.1 us (8%)
  starting transfers between devices  18.2 us (7%)
  matrix products  14.7 us (6%)
  waiting for transfers between devices  9.11 us (3%)
  other arithmetic  8.55 us (3%)
    all_gather x6, blocking collectives, columns(): return lax.all_gather(normed_rows, 'feat', axis=1, tiled=True)  85.9 us
    all_gather x3, blocking collectives, section(): attention = add_heads(lax.all_gather(head_out, 'feat', axis=1, tiled=True))  48.9 us
    all_gather x3, blocking collectives, section(): writes = add_writes(lax.all_gather(block_feats, 'feat', axis=1, tiled=True))  36 us
    psum x6, blocking collectives, halves(): return lax.psum(partial_sum, 'tok')  21.1 us
    ppermute x6, starting transfers between devices, passed_along(): lax.ppermute(value, axis, [(source, source + steps) for source in range(i...  18.2 us
    ppermute x6, waiting for transfers between devices, passed_along(): lax.ppermute(value, axis, [(source, source + steps) for source in range(i...  9.11 us
    unnamed x19, local copies, waits for them, and re-layouts  8.06 us
  transfers between devices with their start and end apart: 6, of which 3 were waited for; matrix products, arithmetic and copies ran while one was open for 2% of the time, Pallas kernels for 0%

commit v1 on v0

--- a/solution.py
+++ b/solution.py
@@ -15,7 +15,7 @@
 
 
 def halves(partial_sum):
-    return lax.psum(partial_sum, "tok")
+    return jnp.sum(lax.all_gather(partial_sum, "tok"), axis=0)
 
 
 def pick_block(lookup_table, chosen, block_len):

time: 266 us -> 256 us (0.962)
  blocking collectives: 192 us -> 181 us
    psum x6 -> x0, blocking collectives: 21.1 us -> none  [halves(): return lax.psum(partial_sum, 'tok')]
    all_gather x0 -> x6, blocking collectives: none -> 11.3 us  [halves(): return jnp.sum(lax.all_gather(partial_sum, 'tok'), axis=0)]
where the time goes in v1:
time: 256 us; the launch traced here: 255 us
  blocking collectives  181 us (71%)
  local copies, waits for them, and re-layouts  21 us (8%)
  starting transfers between devices  18.3 us (7%)
  matrix products  14.7 us (6%)
  waiting for transfers between devices  9.11 us (4%)
  other arithmetic  8.6 us (3%)
    all_gather x6, blocking collectives, columns(): return lax.all_gather(normed_rows, 'feat', axis=1, tiled=True)  85.9 us
    all_gather x3, blocking collectives, section(): attention = add_heads(lax.all_gather(head_out, 'feat', axis=1, tiled=True))  48.3 us
    all_gather x3, blocking collectives, section(): writes = add_writes(lax.all_gather(block_feats, 'feat', axis=1, tiled=True))  36 us
    ppermute x6, starting transfers between devices, passed_along(): lax.ppermute(value, axis, [(source, source + steps) for source in range(i...  18.3 us
    all_gather x6, blocking collectives, halves(): return jnp.sum(lax.all_gather(partial_sum, 'tok'), axis=0)  11.3 us
    ppermute x6, waiting for transfers between devices, passed_along(): lax.ppermute(value, axis, [(source, source + steps) for source in range(i...  9.11 us
    unnamed x19, local copies, waits for them, and re-layouts  8.06 us
  transfers between devices with their start and end apart: 6, of which 3 were waited for; matrix products, arithmetic and copies ran while one was open for 2% of the time, Pallas kernels for 0%

profile of v1, /device:TPU:0, one launch (start us, length us, event | category | flops | bytes accessed | tf_op | source)
XLA Modules:
  0.0 255.0 jit_solution(11428508432403045698)
XLA Ops:
  0.7 0.9 copy-done
  2.2 0.7 fusion.19
  3.0 0.7 select_reduce_fusion
  3.7 6.1 %copy.43 = bf16[1,4,256,2,1,448]{5,3,2,1,4,0:T(2,128)(2,1)} copy(bf16[1,4,256,2,1,448]{2,5,4,3,1,0:T(8,128)(2,1)} %param.23) | data formatting | bytes 3670016 | tf_op args[6]
  9.9 3.5 %reshape_squeeze.9 = bf16[2048,448]{1,0:T(8,128)(2,1)S(1)} reshape(bf16[1,4,256,2,1,448]{5,3,2,1,4,0:T(2,128)(2,1)} %copy.43) | data formatting | bytes 3670016 | tf_op jit(solution)/shard_map/reshape;squeeze | solution.py:61
  13.5 0.8 copy.44
  14.4 0.7 broadcast.116
  15.1 0.7 broadcast_in_dim.131
  15.9 237.3 %while.23 = (s32[]{:T(128)}, f32[64,448]{1,0:T(8,128)S(1)}, f32[2,64,448]{2,1,0:T(8,128)}, f32[128,448]{1,0:T(8,128)}, bf16[128,128]{1,0:T(8,128)(2,1)S(1)}, /*i...) while((s32[]{:T(128)}, f32[64,448]{1,0:T(8,128)S(1)}, ...), condition=%wide.region_4.5_spmd.clone.clone, body=%wide.region_1.4_spmd.clone.clone.sunk | while | flops 268976448 | bytes 12126045 | solution.py:150
  16.1 15.7 %all-gather.12 = bf16[4,448,64]{1,2,0:T(8,128)(2,1)S(1)} all-gather(bf16[1,448,64]{1,2,0:T(8,128)(2,1)S(1)} %fusion.57), channel_id=1, replica_groups=mesh['groups'=2,'feat'=4,'layer'=2,'tok'=2] {'feat'}, dimensions={0}, use_global_device_ids=true | all-gather | bytes 286720 | tf_op jit(solution)/shard_map/while/body/eval_jaxpr/all_gather | solution.py:14
  31.9 0.3 reshape.89
  32.2 1.5 fusion.58
  33.7 1.9 all-gather.13
  35.6 0.6 dynamic_slice.163
  36.2 0.7 iota_compare_fusion.4
  37.2 16.4 %all_gather.92 = bf16[64,2048]{0,1:T(8,128)(2,1)S(1)} all-gather(bf16[64,512]{0,1:T(8,128)(2,1)S(1)} %bitcast.107), channel_id=1, replica_groups=mesh['groups'=2,'feat'=4,'layer'=2,'tok'=2] {'feat'}, dimensions={1}, use_global_device_ids=true | all-gather | bytes 327680 | tf_op jit(solution)/shard_map/while/body/eval_jaxpr/all_gather | solution.py:113
  53.7 0.5 convolution_add_fusion.2
  54.3 14.5 %all-gather.14 = bf16[4,448,64]{1,2,0:T(8,128)(2,1)S(1)} all-gather(bf16[1,448,64]{1,2,0:T(8,128)(2,1)S(1)} %fusion.61), channel_id=1, replica_groups=mesh['groups'=2,'feat'=4,'layer'=2,'tok'=2] {'feat'}, dimensions={0}, use_global_device_ids=true | all-gather | bytes 286720 | tf_op jit(solution)/shard_map/while/body/eval_jaxpr/all_gather | solution.py:14
  69.0 0.3 reshape.90
  69.3 1.2 fusion.62
  70.5 1.9 all-gather.15
  72.5 12.0 %all_gather.93 = bf16[64,512]{1,0:T(8,128)(2,1)S(1)} all-gather(bf16[64,128]{1,0:T(8,128)(2,1)S(1)} %get-tuple-element.762), channel_id=1, replica_groups=mesh['groups'=2,'feat'=4,'layer'=2,'tok'=2] {'feat'}, dimensions={1}, use_global_device_ids=true | all-gather | bytes 81920 | tf_op jit(solution)/shard_map/while/body/eval_jaxpr/all_gather | solution.py:125
  84.5 1.6 fusion.63
  86.1 4.1 %collective-permute-start.1 = (f32[2,64,448]{2,1,0:T(8,128)S(1)}, f32[2,64,448]{2,1,0:T(8,128)}, u32[]{:S(2)}, u32[]{:S(2)}) collective-permute-start(f32[2,64,448]{2,1,0:T(8,128)S(1)} %fusion.63), channel_id=1, source_target_pairs={{0,2},{1,3},{4,6},{5,7},{8,10},{9,11},{12,14},{13,15},{16,18},{17,... | collective-permute-start | bytes 688136 | tf_op jit(solution)/shard_map/while/body/eval_jaxpr/ppermute | solution.py:10
  90.2 1.6 select_dynamic-update-slice_fusion.5
  91.8 1.3 collective-permute-start
  93.1 3.0 %collective-permute-done = f32[64,448]{1,0:T(8,128)S(1)} collective-permute-done((f32[64,448]{1,0:T(8,128)S(1)}, f32[64,448]{1,0:T(8,128)S(1)}, u32[]{:S(2)}, u32[]{:S(2)}) %collective-permute-start) | collective-permute-done | bytes 114720 | tf_op jit(solution)/shard_map/while/body/eval_jaxpr/ppermute | solution.py:10
  96.3 14.3 %all-gather.12 = bf16[4,448,64]{1,2,0:T(8,128)(2,1)S(1)} all-gather(bf16[1,448,64]{1,2,0:T(8,128)(2,1)S(1)} %fusion.57), channel_id=1, replica_groups=mesh['groups'=2,'feat'=4,'layer'=2,'tok'=2] {'feat'}, dimensions={0}, use_global_device_ids=true | all-gather | bytes 286720 | tf_op jit(solution)/shard_map/while/body/eval_jaxpr/all_gather | solution.py:14
  110.8 0.3 reshape.89
  111.1 1.5 fusion.58
  112.6 1.9 all-gather.13
  114.5 0.6 dynamic_slice.163
  115.1 0.7 iota_compare_fusion.4
  116.1 15.9 %all_gather.92 = bf16[64,2048]{0,1:T(8,128)(2,1)S(1)} all-gather(bf16[64,512]{0,1:T(8,128)(2,1)S(1)} %bitcast.107), channel_id=1, replica_groups=mesh['groups'=2,'feat'=4,'layer'=2,'tok'=2] {'feat'}, dimensions={1}, use_global_device_ids=true | all-gather | bytes 327680 | tf_op jit(solution)/shard_map/while/body/eval_jaxpr/all_gather | solution.py:113
  132.1 0.5 convolution_add_fusion.2
  132.7 13.8 %all-gather.14 = bf16[4,448,64]{1,2,0:T(8,128)(2,1)S(1)} all-gather(bf16[1,448,64]{1,2,0:T(8,128)(2,1)S(1)} %fusion.61), channel_id=1, replica_groups=mesh['groups'=2,'feat'=4,'layer'=2,'tok'=2] {'feat'}, dimensions={0}, use_global_device_ids=true | all-gather | bytes 286720 | tf_op jit(solution)/shard_map/while/body/eval_jaxpr/all_gather | solution.py:14
  146.8 0.3 reshape.90
  147.0 1.2 fusion.62
  148.3 1.9 all-gather.15
  150.2 12.0 %all_gather.93 = bf16[64,512]{1,0:T(8,128)(2,1)S(1)} all-gather(bf16[64,128]{1,0:T(8,128)(2,1)S(1)} %get-tuple-element.762), channel_id=1, replica_groups=mesh['groups'=2,'feat'=4,'layer'=2,'tok'=2] {'feat'}, dimensions={1}, use_global_device_ids=true | all-gather | bytes 81920 | tf_op jit(solution)/shard_map/while/body/eval_jaxpr/all_gather | solution.py:125
  162.2 1.6 fusion.63
  163.8 5.2 %collective-permute-start.1 = (f32[2,64,448]{2,1,0:T(8,128)S(1)}, f32[2,64,448]{2,1,0:T(8,128)}, u32[]{:S(2)}, u32[]{:S(2)}) collective-permute-start(f32[2,64,448]{2,1,0:T(8,128)S(1)} %fusion.63), channel_id=1, source_target_pairs={{0,2},{1,3},{4,6},{5,7},{8,10},{9,11},{12,14},{13,15},{16,18},{17,... | collective-permute-start | bytes 688136 | tf_op jit(solution)/shard_map/while/body/eval_jaxpr/ppermute | solution.py:10
  169.0 1.7 select_dynamic-update-slice_fusion.5
  170.6 1.3 collective-permute-start
  171.9 3.0 %collective-permute-done = f32[64,448]{1,0:T(8,128)S(1)} collective-permute-done((f32[64,448]{1,0:T(8,128)S(1)}, f32[64,448]{1,0:T(8,128)S(1)}, u32[]{:S(2)}, u32[]{:S(2)}) %collective-permute-start) | collective-permute-done | bytes 114720 | tf_op jit(solution)/shard_map/while/body/eval_jaxpr/ppermute | solution.py:10
  175.1 13.8 %all-gather.12 = bf16[4,448,64]{1,2,0:T(8,128)(2,1)S(1)} all-gather(bf16[1,448,64]{1,2,0:T(8,128)(2,1)S(1)} %fusion.57), channel_id=1, replica_groups=mesh['groups'=2,'feat'=4,'layer'=2,'tok'=2] {'feat'}, dimensions={0}, use_global_device_ids=true | all-gather | bytes 286720 | tf_op jit(solution)/shard_map/while/body/eval_jaxpr/all_gather | solution.py:14
  189.1 0.3 reshape.89
  189.4 1.4 fusion.58
  190.8 1.9 all-gather.13
  192.7 0.6 dynamic_slice.163
  193.4 0.7 iota_compare_fusion.4
  194.4 16.0 %all_gather.92 = bf16[64,2048]{0,1:T(8,128)(2,1)S(1)} all-gather(bf16[64,512]{0,1:T(8,128)(2,1)S(1)} %bitcast.107), channel_id=1, replica_groups=mesh['groups'=2,'feat'=4,'layer'=2,'tok'=2] {'feat'}, dimensions={1}, use_global_device_ids=true | all-gather | bytes 327680 | tf_op jit(solution)/shard_map/while/body/eval_jaxpr/all_gather | solution.py:113
  210.4 0.5 convolution_add_fusion.2
  211.0 13.8 %all-gather.14 = bf16[4,448,64]{1,2,0:T(8,128)(2,1)S(1)} all-gather(bf16[1,448,64]{1,2,0:T(8,128)(2,1)S(1)} %fusion.61), channel_id=1, replica_groups=mesh['groups'=2,'feat'=4,'layer'=2,'tok'=2] {'feat'}, dimensions={0}, use_global_device_ids=true | all-gather | bytes 286720 | tf_op jit(solution)/shard_map/while/body/eval_jaxpr/all_gather | solution.py:14
  225.0 0.3 reshape.90
  225.3 1.2 fusion.62
  226.5 1.9 all-gather.15
  228.5 12.0 %all_gather.93 = bf16[64,512]{1,0:T(8,128)(2,1)S(1)} all-gather(bf16[64,128]{1,0:T(8,128)(2,1)S(1)} %get-tuple-element.762), channel_id=1, replica_groups=mesh['groups'=2,'feat'=4,'layer'=2,'tok'=2] {'feat'}, dimensions={1}, use_global_device_ids=true | all-gather | bytes 81920 | tf_op jit(solution)/shard_map/while/body/eval_jaxpr/all_gather | solution.py:125
  240.5 1.6 fusion.63
  242.1 5.2 %collective-permute-start.1 = (f32[2,64,448]{2,1,0:T(8,128)S(1)}, f32[2,64,448]{2,1,0:T(8,128)}, u32[]{:S(2)}, u32[]{:S(2)}) collective-permute-start(f32[2,64,448]{2,1,0:T(8,128)S(1)} %fusion.63), channel_id=1, source_target_pairs={{0,2},{1,3},{4,6},{5,7},{8,10},{9,11},{12,14},{13,15},{16,18},{17,... | collective-permute-start | bytes 688136 | tf_op jit(solution)/shard_map/while/body/eval_jaxpr/ppermute | solution.py:10
  247.2 1.7 select_dynamic-update-slice_fusion.5
  248.9 1.3 collective-permute-start
  250.2 3.0 %collective-permute-done = f32[64,448]{1,0:T(8,128)S(1)} collective-permute-done((f32[64,448]{1,0:T(8,128)S(1)}, f32[64,448]{1,0:T(8,128)S(1)}, u32[]{:S(2)}, u32[]{:S(2)}) %collective-permute-start) | collective-permute-done | bytes 114720 | tf_op jit(solution)/shard_map/while/body/eval_jaxpr/ppermute | solution.py:10
  253.2 1.8 copy.45
  (61 shorter events, 3.6 us)
Async XLA Ops:
  0.6 1.0 copy-start
  9.8 3.5 %copy-start.2 = (f32[128,1,448]{0,2,1:T(8,128)S(1)}, f32[128,1,448]{0,2,1:T(8,128)}, u32[]{:S(2)}) copy-start(f32[128,1,448]{0,2,1:T(8,128)} %param.17) | copy-start | bytes 688132
  9.8 3.7 %copy-start.3 = (f32[1,128,1,448]{1,3,2,0:T(8,128)S(1)}, f32[1,128,1,448]{1,3,2,0:T(8,128)}, u32[]{:S(2)}) copy-start(f32[1,128,1,448]{1,3,2,0:T(8,128)} %param.27) | copy-start | bytes 688132
  9.8 6.0 %copy-start.4 = (f32[1,128]{1,0:T(1,128)S(1)}, f32[1,128]{1,0:T(1,128)}, u32[]{:S(2)}) copy-start(f32[1,128]{1,0:T(1,128)} %param.25) | copy-start | bytes 1540
  9.8 6.0 %copy-start.5 = (f32[1,128]{1,0:T(1,128)S(1)}, f32[1,128]{1,0:T(1,128)}, u32[]{:S(2)}) copy-start(f32[1,128]{1,0:T(1,128)} %param.18) | copy-start | bytes 1540
  9.9 6.0 %copy-start.6 = (s32[2]{0:T(128)S(1)}, s32[2]{0:T(128)}, u32[]{:S(2)}) copy-start(s32[2]{0:T(128)} %param.21) | copy-start | bytes 28
  9.9 6.0 %copy-start.7 = (f32[1,128]{1,0:T(1,128)S(1)}, f32[1,128]{1,0:T(1,128)}, u32[]{:S(2)}) copy-start(f32[1,128]{1,0:T(1,128)} %param.19) | copy-start | bytes 1540
  86.1 10.1 %collective-permute-start.1 = (f32[2,64,448]{2,1,0:T(8,128)S(1)}, f32[2,64,448]{2,1,0:T(8,128)}, u32[]{:S(2)}, u32[]{:S(2)}) collective-permute-start(f32[2,64,448]{2,1,0:T(8,128)S(1)} %fusion.63), channel_id=1, source_target_pairs={{0,2},{1,3},{4,6},{5,7},{8,10},{9,11},{12,14},{13,15},{16,18},{17,... | collective-permute-start | bytes 688136 | tf_op jit(solution)/shard_map/while/body/eval_jaxpr/ppermute | solution.py:10
  91.8 4.3 %collective-permute-start = (f32[64,448]{1,0:T(8,128)S(1)}, f32[64,448]{1,0:T(8,128)S(1)}, u32[]{:S(2)}, u32[]{:S(2)}) collective-permute-start(f32[64,448]{1,0:T(8,128)S(1)} %get-tuple-element.763), channel_id=1, source_target_pairs={{0,2},{1,3},{4,6},{5,7},{8,10},{9,11},{12,14},{13,15},{16,18},{17,... | collective-permute-start | bytes 344072 | tf_op jit(solution)/shard_map/while/body/eval_jaxpr/ppermute | solution.py:10
  163.8 11.2 %collective-permute-start.1 = (f32[2,64,448]{2,1,0:T(8,128)S(1)}, f32[2,64,448]{2,1,0:T(8,128)}, u32[]{:S(2)}, u32[]{:S(2)}) collective-permute-start(f32[2,64,448]{2,1,0:T(8,128)S(1)} %fusion.63), channel_id=1, source_target_pairs={{0,2},{1,3},{4,6},{5,7},{8,10},{9,11},{12,14},{13,15},{16,18},{17,... | collective-permute-start | bytes 688136 | tf_op jit(solution)/shard_map/while/body/eval_jaxpr/ppermute | solution.py:10
  170.6 4.3 %collective-permute-start = (f32[64,448]{1,0:T(8,128)S(1)}, f32[64,448]{1,0:T(8,128)S(1)}, u32[]{:S(2)}, u32[]{:S(2)}) collective-permute-start(f32[64,448]{1,0:T(8,128)S(1)} %get-tuple-element.763), channel_id=1, source_target_pairs={{0,2},{1,3},{4,6},{5,7},{8,10},{9,11},{12,14},{13,15},{16,18},{17,... | collective-permute-start | bytes 344072 | tf_op jit(solution)/shard_map/while/body/eval_jaxpr/ppermute | solution.py:10
  242.1 11.1 %collective-permute-start.1 = (f32[2,64,448]{2,1,0:T(8,128)S(1)}, f32[2,64,448]{2,1,0:T(8,128)}, u32[]{:S(2)}, u32[]{:S(2)}) collective-permute-start(f32[2,64,448]{2,1,0:T(8,128)S(1)} %fusion.63), channel_id=1, source_target_pairs={{0,2},{1,3},{4,6},{5,7},{8,10},{9,11},{12,14},{13,15},{16,18},{17,... | collective-permute-start | bytes 688136 | tf_op jit(solution)/shard_map/while/body/eval_jaxpr/ppermute | solution.py:10
  248.9 4.3 %collective-permute-start = (f32[64,448]{1,0:T(8,128)S(1)}, f32[64,448]{1,0:T(8,128)S(1)}, u32[]{:S(2)}, u32[]{:S(2)}) collective-permute-start(f32[64,448]{1,0:T(8,128)S(1)} %get-tuple-element.763), channel_id=1, source_target_pairs={{0,2},{1,3},{4,6},{5,7},{8,10},{9,11},{12,14},{13,15},{16,18},{17,... | collective-permute-start | bytes 344072 | tf_op jit(solution)/shard_map/while/body/eval_jaxpr/ppermute | solution.py:10
  253.2 1.8 copy-start.1
